TPU v7x, 512 devices: a whole 4x8x8 slice. The times are simulated.
512 devices in a mesh: band: 32 (over z_lo, y, core), dom: 16 (over z_hi, x).
Axes of the slice: x: 4, y: 8, z: 8 (z_hi: 4, z_lo: 2; z = z_hi * 2 + z_lo), core: 2. Of those that a mesh axis runs over, the one named last changes fastest.
Arguments:
- states: float32 [4096, 8, 128, 128], P('band', None, 'dom'), may hold values from -0.015625 to 0.015625
- window: float32 [128, 8, 128, 128], P('band', None, 'dom'), may hold values from -6 to 6
- potential: float32 [8, 128, 128], P(None, 'dom'), may hold values from -3 to 3
Outputs:
- intersection: float32 [4096, 128], P('band')
- hamiltonian: float32 [4096, 128], P('band')
All inputs are finite; a program needn't handle non-finite values.
Results may differ from a plain program's by a relative error of at most 0.00012.
Values sent between devices are 32-bit elements; how exact they have to be, the bound alone decides.
A program may use at most 64 MiB of HBM per device.

v0:
```python
import jax
import jax.numpy as jnp
from jax import lax
from jax.sharding import PartitionSpec as P

DEGREE = 4


coeffs = (
    -5369.0 / 1800.0,
    12.0 / 7.0,
    -15.0 / 56.0,
    10.0 / 189.0,
    -1.0 / 112.0,
    2.0 / 1925.0,
    -1.0 / 16632.0,
)
centre_value = 9.0
half_width = 7.0


def padded(block, sides, width):
    for axis, dim in sides:
        count = lax.axis_size(axis)
        forward = [(i, i + 1) for i in range(count - 1)]
        forward.append((count - 1, 0))
        backward = [(target, source) for source, target in forward]
        low = lax.ppermute(
            lax.slice_in_dim(block, block.shape[dim] - width, None, axis=dim), axis, forward
        )
        high = lax.ppermute(lax.slice_in_dim(block, 0, width, axis=dim), axis, backward)
        block = jnp.concatenate([low, block, high], axis=dim)
    return block


def stencil_sum(wave_in, padded_x, padded_y, potential):
    x_cells = wave_in.shape[2]
    y_cells = wave_in.shape[3]
    z_cells = wave_in.shape[1]
    along_z = jnp.pad(wave_in, ((0, 0), (6, 6), (0, 0), (0, 0)))
    laplace = 3.0 * coeffs[0] * wave_in
    for offset in range(1, 7):
        beside = (
            padded_x[:, :, 6 + offset : 6 + offset + x_cells]
            + padded_x[:, :, 6 - offset : 6 - offset + x_cells]
        )
        beside = (
            beside
            + padded_y[:, :, :, 6 + offset : 6 + offset + y_cells]
            + padded_y[:, :, :, 6 - offset : 6 - offset + y_cells]
        )
        beside = (
            beside
            + along_z[:, 6 + offset : 6 + offset + z_cells]
            + along_z[:, 6 - offset : 6 - offset + z_cells]
        )
        laplace = laplace + coeffs[offset] * beside
    return -0.5 * laplace + potential * wave_in


def apply_banded(wave_in, potential):
    padded_x = padded(wave_in, (("dom", 2),), 6)
    padded_y = jnp.concatenate((wave_in[:, :, :, -6:], wave_in, wave_in[:, :, :, :6]), axis=3)
    return stencil_sum(wave_in, padded_x, padded_y, potential)


def chebyshev(window, operate):
    previous = window
    current = (operate(window) - centre_value * window) / half_width
    for repeat_index in range(DEGREE - 1):
        following = 2.0 * (operate(current) - centre_value * current) / half_width - previous
        previous, current = (current, following)
    image = operate(current)
    return jnp.stack((current, image))


def per_device(states, window, potential):
    stacked = chebyshev(window, lambda wave: apply_banded(wave, potential))
    states_flat = states.reshape(states.shape[0], -1)
    whole_window = lax.all_gather(stacked, "band", axis=1, tiled=True)
    flat_piece = whole_window.reshape(-1, states_flat.shape[1])
    product = lax.dot_general(
        states_flat,
        flat_piece,
        (((1,), (1,)), ((), ())),
        precision=lax.Precision.HIGHEST,
        preferred_element_type=jnp.float32,
    )
    partial_value = product.reshape(states_flat.shape[0], 2, whole_window.shape[1])
    totals = lax.psum(partial_value, "dom")
    return (totals[:, 0, :], totals[:, 1, :])


def solution(mesh):
    in_specs = (P("band", None, "dom", None), P("band", None, "dom", None), P(None, "dom", None))
    out_specs = (P("band", None), P("band", None))
    return jax.shard_map(
        per_device, mesh=mesh, in_specs=in_specs, out_specs=out_specs, check_vma=False
    )
```

profile of v0, /device:TPU:16, one launch (start us, length us, event | category | flops | bytes accessed | tf_op | source)
XLA Modules:
  0.0 371.6 jit_solution(3588212571015930287)
XLA Ops:
  7.2 0.0 copy-start
  7.2 0.0 all-gather.2.cloned.1.call-start
  7.2 1.0 fusion.338
  8.2 13.1 %collective-permute-start = (f32[4,8,6,128]{3,2,1,0:T(8,128)S(1)}, f32[4,8,6,128]{3,2,1,0:T(8,128)S(1)}, u32[]{:S(2)}, u32[]{:S(2)}) collective-permute-start(f32[4,8,6,128]{3,2,1,0:T(8,128)S(1)} %get-tuple-element.22), channel_id=1, source_target_pairs={{1,0},{2,1},{3,2},{4,3},{5,4},{6,5},{7,6},{8,7},{9,8},{10,9},{11,1... | collective-permute-start | bytes 294920 | tf_op jit(solution)/shard_map/ppermute | solution.py:31
  21.4 1.9 collective-permute-start.1
  23.3 1.1 fusion.339
  24.4 0.8 broadcast_multiply_fusion.1
  25.1 0.9 constant_dynamic-update-slice_fusion.1
  26.1 0.8 collective-permute-done
  26.9 7.5 %collective-permute-done.1 = f32[4,8,6,128]{3,2,1,0:T(8,128)S(1)} collective-permute-done((f32[4,8,6,128]{3,2,1,0:T(8,128)S(1)}, f32[4,8,6,128]{3,2,1,0:T(8,128)S(1)}, u32[]{:S(2)}, u32[]{:S(2)}) %collective-permute-start.1) | collective-permute-done | bytes 98336 | tf_op jit(solution)/shard_map/ppermute | solution.py:28
  34.5 5.2 %broadcast_multiply_fusion = (f32[4,8,8,128]{3,2,1,0:T(8,128)S(1)}, f32[4,8,8,128]{3,2,1,0:T(8,128)S(1)}) fusion(f32[4,8,8,128]{3,2,1,0:T(8,128)} %param.4, f32[8,8,128]{2,1,0:T(8,128)} %param.5, f32[4,8,8,6]{3,2,1,0:T(8,128)S(1)} %get-tuple-element.25, f32[4,8,8,6]{3,2,1,0:T(8,128)S(1)} %get-tuple-element.24, ...), kind=kLoop, calls=%fused_computation.601 | loop fusion | flops 2195456 | bytes 1323008 | tf_op jit(solution)/shard_map/div | solution.py:69
  39.7 1.9 collective-permute-start.2
  41.6 3.9 %collective-permute-start.3 = (f32[4,8,6,128]{3,2,1,0:T(8,128)S(1)}, f32[4,8,6,128]{3,2,1,0:T(8,128)S(1)}, u32[]{:S(2)}, u32[]{:S(2)}) collective-permute-start(f32[4,8,6,128]{3,2,1,0:T(8,128)S(1)} %get-tuple-element.19), channel_id=1, source_target_pairs={{0,1},{1,2},{2,3},{3,4},{4,5},{5,6},{6,7},{7,8},{8,9},{9,10},{10,1... | collective-permute-start | bytes 294920 | tf_op jit(solution)/shard_map/ppermute | solution.py:28
  45.6 0.1 fusion.337
  45.7 1.8 collective-permute-done.2
  47.5 7.0 %collective-permute-done.3 = f32[4,8,6,128]{3,2,1,0:T(8,128)S(1)} collective-permute-done((f32[4,8,6,128]{3,2,1,0:T(8,128)S(1)}, f32[4,8,6,128]{3,2,1,0:T(8,128)S(1)}, u32[]{:S(2)}, u32[]{:S(2)}) %collective-permute-start.3) | collective-permute-done | bytes 98336 | tf_op jit(solution)/shard_map/ppermute | solution.py:28
  54.5 1.8 fusion.195
  56.2 1.9 collective-permute-start.4
  58.2 3.9 %collective-permute-start.5 = (f32[4,8,6,128]{3,2,1,0:T(8,128)S(1)}, f32[4,8,6,128]{3,2,1,0:T(8,128)S(1)}, u32[]{:S(2)}, u32[]{:S(2)}) collective-permute-start(f32[4,8,6,128]{3,2,1,0:T(8,128)S(1)} %get-tuple-element.15), channel_id=1, source_target_pairs={{0,1},{1,2},{2,3},{3,4},{4,5},{5,6},{6,7},{7,8},{8,9},{9,10},{10,1... | collective-permute-start | bytes 294920 | tf_op jit(solution)/shard_map/ppermute | solution.py:28
  62.1 0.1 fusion.335
  62.2 0.9 collective-permute-done.4
  63.1 6.2 %collective-permute-done.5 = f32[4,8,6,128]{3,2,1,0:T(8,128)S(1)} collective-permute-done((f32[4,8,6,128]{3,2,1,0:T(8,128)S(1)}, f32[4,8,6,128]{3,2,1,0:T(8,128)S(1)}, u32[]{:S(2)}, u32[]{:S(2)}) %collective-permute-start.5) | collective-permute-done | bytes 98336 | tf_op jit(solution)/shard_map/ppermute | solution.py:28
  69.3 1.6 fusion.134
  70.9 1.9 collective-permute-start.6
  72.9 3.9 %collective-permute-start.7 = (f32[4,8,6,128]{3,2,1,0:T(8,128)S(1)}, f32[4,8,6,128]{3,2,1,0:T(8,128)S(1)}, u32[]{:S(2)}, u32[]{:S(2)}) collective-permute-start(f32[4,8,6,128]{3,2,1,0:T(8,128)S(1)} %get-tuple-element.11), channel_id=1, source_target_pairs={{0,1},{1,2},{2,3},{3,4},{4,5},{5,6},{6,7},{7,8},{8,9},{9,10},{10,1... | collective-permute-start | bytes 294920 | tf_op jit(solution)/shard_map/ppermute | solution.py:28
  76.8 0.1 fusion.333
  76.9 0.9 collective-permute-done.6
  77.8 6.8 %collective-permute-done.7 = f32[4,8,6,128]{3,2,1,0:T(8,128)S(1)} collective-permute-done((f32[4,8,6,128]{3,2,1,0:T(8,128)S(1)}, f32[4,8,6,128]{3,2,1,0:T(8,128)S(1)}, u32[]{:S(2)}, u32[]{:S(2)}) %collective-permute-start.7) | collective-permute-done | bytes 98336 | tf_op jit(solution)/shard_map/ppermute | solution.py:28
  84.6 0.0 copy-done
  84.6 0.9 fusion.73
  85.5 1.9 collective-permute-start.8
  87.4 3.9 %collective-permute-start.9 = (f32[4,8,6,128]{3,2,1,0:T(8,128)S(1)}, f32[4,8,6,128]{3,2,1,0:T(8,128)S(1)}, u32[]{:S(2)}, u32[]{:S(2)}) collective-permute-start(f32[4,8,6,128]{3,2,1,0:T(8,128)S(1)} %get-tuple-element.7), channel_id=1, source_target_pairs={{0,1},{1,2},{2,3},{3,4},{4,5},{5,6},{6,7},{7,8},{8,9},{9,10},{10,1... | collective-permute-start | bytes 294920 | tf_op jit(solution)/shard_map/ppermute | solution.py:28
  91.3 0.1 fusion.331
  91.4 0.9 collective-permute-done.8
  92.3 6.1 %collective-permute-done.9 = f32[4,8,6,128]{3,2,1,0:T(8,128)S(1)} collective-permute-done((f32[4,8,6,128]{3,2,1,0:T(8,128)S(1)}, f32[4,8,6,128]{3,2,1,0:T(8,128)S(1)}, u32[]{:S(2)}, u32[]{:S(2)}) %collective-permute-start.9) | collective-permute-done | bytes 98336 | tf_op jit(solution)/shard_map/ppermute | solution.py:28
  98.5 0.9 fusion.12
  99.3 0.7 pad_maximum_fusion
  100.1 0.0 all-gather.2.cloned.1.call-update
  100.1 0.0 all-reduce.7.cloned.1.call-start
  100.1 69.9 %all-gather.2.cloned.1.call-done = f32[2,128,8,8,128]{4,3,2,1,0:T(8,128)} async-done(((f32[2,4,8,8,128]{4,3,2,1,0:T(8,128)}), f32[2,128,8,8,128]{4,3,2,1,0:T(8,128)}) %all-gather.2.cloned.1.call-update) | async-done | bytes 8388624 | tf_op jit(solution)/shard_map/all_gather | solution.py:80
  170.0 9.4 %reshape.14 = f32[256,8192]{1,0:T(8,128)} reshape(f32[2,128,8,8,128]{4,3,2,1,0:T(8,128)} %all-gather.2.cloned.1.call-done) | data formatting | bytes 16777216 | tf_op jit(solution)/shard_map/reshape | solution.py:81
  179.4 11.7 %fusion = f32[256,128]{1,0:T(8,128)S(1)} fusion(f32[256,8192]{1,0:T(8,128)} %reshape.14, f32[16,8,64,128]{3,2,1,0:T(8,128)} %bitcast.19), kind=kOutput, calls=%fused_computation | convolution fusion | flops 3221225472 | bytes 12713984 | tf_op jit(solution)/shard_map/dot_general | solution.py:82
  191.1 0.7 copy.5
  191.9 0.0 all-reduce.7.cloned.1.call-update
  191.9 171.4 %all-reduce.7.cloned.1.call-done = f32[128,2,128]{2,0,1:T(8,128)} async-done(((f32[128,2,128]{2,0,1:T(8,128)}), f32[128,2,128]{2,0,1:T(8,128)}) %all-reduce.7.cloned.1.call-update) | async-done | bytes 131088 | tf_op jit(solution)/shard_map/psum | solution.py:90
  363.3 1.5 slice_bitcast_fusion
  (5 shorter events, 0.1 us)
Async XLA Ops:
  7.2 77.4 %copy-start = (f32[8,8,128]{2,1,0:T(8,128)S(1)}, f32[8,8,128]{2,1,0:T(8,128)}, u32[]{:S(2)}) copy-start(f32[8,8,128]{2,1,0:T(8,128)} %param.5) | copy-start | bytes 98308
  7.2 162.9 %all-gather.2.cloned.1.call-start = ((), (), s32[]{:S(2)}) async-start(), calls=%async_computation | async-start | bytes 8650752 | tf_op jit(solution)/shard_map/all_gather | solution.py:80
  8.2 18.7 %collective-permute-start = (f32[4,8,6,128]{3,2,1,0:T(8,128)S(1)}, f32[4,8,6,128]{3,2,1,0:T(8,128)S(1)}, u32[]{:S(2)}, u32[]{:S(2)}) collective-permute-start(f32[4,8,6,128]{3,2,1,0:T(8,128)S(1)} %get-tuple-element.22), channel_id=1, source_target_pairs={{1,0},{2,1},{3,2},{4,3},{5,4},{6,5},{7,6},{8,7},{9,8},{10,9},{11,1... | collective-permute-start | bytes 294920 | tf_op jit(solution)/shard_map/ppermute | solution.py:31
  21.4 13.1 %collective-permute-start.1 = (f32[4,8,6,128]{3,2,1,0:T(8,128)S(1)}, f32[4,8,6,128]{3,2,1,0:T(8,128)S(1)}, u32[]{:S(2)}, u32[]{:S(2)}) collective-permute-start(f32[4,8,6,128]{3,2,1,0:T(8,128)S(1)} %get-tuple-element.23), channel_id=1, source_target_pairs={{0,1},{1,2},{2,3},{3,4},{4,5},{5,6},{6,7},{7,8},{8,9},{9,10},{10,1... | collective-permute-start | bytes 294920 | tf_op jit(solution)/shard_map/ppermute | solution.py:28
  39.7 7.8 %collective-permute-start.2 = (f32[4,8,6,128]{3,2,1,0:T(8,128)S(1)}, f32[4,8,6,128]{3,2,1,0:T(8,128)S(1)}, u32[]{:S(2)}, u32[]{:S(2)}) collective-permute-start(f32[4,8,6,128]{3,2,1,0:T(8,128)S(1)} %get-tuple-element.18), channel_id=1, source_target_pairs={{1,0},{2,1},{3,2},{4,3},{5,4},{6,5},{7,6},{8,7},{9,8},{10,9},{11,1... | collective-permute-start | bytes 294920 | tf_op jit(solution)/shard_map/ppermute | solution.py:31
  41.6 12.8 %collective-permute-start.3 = (f32[4,8,6,128]{3,2,1,0:T(8,128)S(1)}, f32[4,8,6,128]{3,2,1,0:T(8,128)S(1)}, u32[]{:S(2)}, u32[]{:S(2)}) collective-permute-start(f32[4,8,6,128]{3,2,1,0:T(8,128)S(1)} %get-tuple-element.19), channel_id=1, source_target_pairs={{0,1},{1,2},{2,3},{3,4},{4,5},{5,6},{6,7},{7,8},{8,9},{9,10},{10,1... | collective-permute-start | bytes 294920 | tf_op jit(solution)/shard_map/ppermute | solution.py:28
  56.2 6.9 %collective-permute-start.4 = (f32[4,8,6,128]{3,2,1,0:T(8,128)S(1)}, f32[4,8,6,128]{3,2,1,0:T(8,128)S(1)}, u32[]{:S(2)}, u32[]{:S(2)}) collective-permute-start(f32[4,8,6,128]{3,2,1,0:T(8,128)S(1)} %get-tuple-element.14), channel_id=1, source_target_pairs={{1,0},{2,1},{3,2},{4,3},{5,4},{6,5},{7,6},{8,7},{9,8},{10,9},{11,1... | collective-permute-start | bytes 294920 | tf_op jit(solution)/shard_map/ppermute | solution.py:31
  58.2 11.1 %collective-permute-start.5 = (f32[4,8,6,128]{3,2,1,0:T(8,128)S(1)}, f32[4,8,6,128]{3,2,1,0:T(8,128)S(1)}, u32[]{:S(2)}, u32[]{:S(2)}) collective-permute-start(f32[4,8,6,128]{3,2,1,0:T(8,128)S(1)} %get-tuple-element.15), channel_id=1, source_target_pairs={{0,1},{1,2},{2,3},{3,4},{4,5},{5,6},{6,7},{7,8},{8,9},{9,10},{10,1... | collective-permute-start | bytes 294920 | tf_op jit(solution)/shard_map/ppermute | solution.py:28
  70.9 6.9 %collective-permute-start.6 = (f32[4,8,6,128]{3,2,1,0:T(8,128)S(1)}, f32[4,8,6,128]{3,2,1,0:T(8,128)S(1)}, u32[]{:S(2)}, u32[]{:S(2)}) collective-permute-start(f32[4,8,6,128]{3,2,1,0:T(8,128)S(1)} %get-tuple-element.10), channel_id=1, source_target_pairs={{1,0},{2,1},{3,2},{4,3},{5,4},{6,5},{7,6},{8,7},{9,8},{10,9},{11,1... | collective-permute-start | bytes 294920 | tf_op jit(solution)/shard_map/ppermute | solution.py:31
  72.9 11.7 %collective-permute-start.7 = (f32[4,8,6,128]{3,2,1,0:T(8,128)S(1)}, f32[4,8,6,128]{3,2,1,0:T(8,128)S(1)}, u32[]{:S(2)}, u32[]{:S(2)}) collective-permute-start(f32[4,8,6,128]{3,2,1,0:T(8,128)S(1)} %get-tuple-element.11), channel_id=1, source_target_pairs={{0,1},{1,2},{2,3},{3,4},{4,5},{5,6},{6,7},{7,8},{8,9},{9,10},{10,1... | collective-permute-start | bytes 294920 | tf_op jit(solution)/shard_map/ppermute | solution.py:28
  85.5 6.9 %collective-permute-start.8 = (f32[4,8,6,128]{3,2,1,0:T(8,128)S(1)}, f32[4,8,6,128]{3,2,1,0:T(8,128)S(1)}, u32[]{:S(2)}, u32[]{:S(2)}) collective-permute-start(f32[4,8,6,128]{3,2,1,0:T(8,128)S(1)} %get-tuple-element.6), channel_id=1, source_target_pairs={{1,0},{2,1},{3,2},{4,3},{5,4},{6,5},{7,6},{8,7},{9,8},{10,9},{11,1... | collective-permute-start | bytes 294920 | tf_op jit(solution)/shard_map/ppermute | solution.py:31
  87.4 11.1 %collective-permute-start.9 = (f32[4,8,6,128]{3,2,1,0:T(8,128)S(1)}, f32[4,8,6,128]{3,2,1,0:T(8,128)S(1)}, u32[]{:S(2)}, u32[]{:S(2)}) collective-permute-start(f32[4,8,6,128]{3,2,1,0:T(8,128)S(1)} %get-tuple-element.7), channel_id=1, source_target_pairs={{0,1},{1,2},{2,3},{3,4},{4,5},{5,6},{6,7},{7,8},{8,9},{9,10},{10,1... | collective-permute-start | bytes 294920 | tf_op jit(solution)/shard_map/ppermute | solution.py:28
  100.1 263.2 %all-reduce.7.cloned.1.call-start = ((), (), s32[]{:S(2)}) async-start(), calls=%async_computation.1 | async-start | bytes 262144 | tf_op jit(solution)/shard_map/psum | solution.py:90
Sparse Core Ops, SparseCore 0:
  100.2 69.7 all-gather.1
  192.0 171.2 all-reduce.6
where the time goes:
time: 373 us; the launch traced here: 372 us
  waiting for transfers between devices  280 us (75%)
  starting transfers between devices  38.5 us (10%)
  local copies, waits for them, and re-layouts  15.1 us (4%)
  between operations  14.2 us (4%)
  other arithmetic  11.8 us (3%)
  matrix products  11.7 us (3%)
    psum x1, waiting for transfers between devices, per_device(): totals = lax.psum(partial_value, 'dom')  171 us
    all_gather x1, waiting for transfers between devices, per_device(): whole_window = lax.all_gather(stacked, 'band', axis=1, tiled=True)  69.9 us
    ppermute x5, waiting for transfers between devices, padded(): lax.ppermute(lax.slice_in_dim(block, block.shape[dim] - width, None, axis...  33.6 us
    ppermute x5, starting transfers between devices, padded(): lax.ppermute(lax.slice_in_dim(block, 0, width, axis=dim), axis, backward)  20.8 us
    ppermute x5, starting transfers between devices, padded(): lax.ppermute(lax.slice_in_dim(block, block.shape[dim] - width, None, axis...  17.6 us
    dot_general x1, matrix products, per_device(): lax.dot_general(states_flat, flat_piece, (((1,), (1,)), ((), ())), precis...  11.7 us
    reshape x1, local copies, waits for them, and re-layouts, per_device(): flat_piece = whole_window.reshape(-1, states_flat.shape[1])  9.36 us
  transfers between devices with their start and end apart: 12, of which 12 were waited for; matrix products, arithmetic and copies ran while one was open for 1% of the time, Pallas kernels for 0%

commit v1 on v0

v1 whole, which is shorter than its diff:
```python
import jax
import jax.numpy as jnp
from jax import lax
from jax.experimental import pallas as pl
from jax.experimental.pallas import tpu as pltpu
from jax.sharding import PartitionSpec as P

COEFFS = (
    -5369.0 / 1800.0,
    12.0 / 7.0,
    -15.0 / 56.0,
    10.0 / 189.0,
    -1.0 / 112.0,
    2.0 / 1925.0,
    -1.0 / 16632.0,
)
CENTRE = 9.0
HALF_WIDTH = 7.0
MESH = pl.DeviceIdType.MESH
NY = 128
NZ = 8
TILE = 8
XN = 4
HN = 4
YN = 8
SPAN = 96
CELLS = 4096


def apply_h(source, potential, z, low, high):
    value = source[z, low:high, :]
    total = (3.0 * COEFFS[0]) * value
    for k in range(1, 7):
        beside = source[z, low + k : high + k, :] + source[z, low - k : high - k, :]
        beside = beside + pltpu.roll(value, k, 1) + pltpu.roll(value, NY - k, 1)
        if z + k < NZ:
            beside = beside + source[z + k, low:high, :]
        if z - k >= 0:
            beside = beside + source[z - k, low:high, :]
        total = total + COEFFS[k] * beside
    return -0.5 * total + potential[z, low:high, :] * value, value


def kernel(
    states, window, potential, out_f, out_h,
    even, odd, pot, image, pieces, rows, high, low, gathered, left, partial, parts, whole,
    send_w, recv_w, send_p, recv_p, local, send_s, recv_s, send_b, recv_b,
    send_up, send_down, send_z, recv_g, send_r, recv_r, send_o, recv_o,
):
    b = lax.axis_index("band")
    d = lax.axis_index("dom")
    c = lax.rem(b, 2)
    q = lax.div(b, 2)
    y = lax.rem(q, YN)
    zl = lax.div(q, YN)
    x = lax.rem(d, XN)
    h = lax.div(d, XN)

    def band_of(chip, core):
        return chip * 2 + core

    def chip_at(lo, offset):
        return lo * YN + lax.rem(y + offset + YN, YN)

    up = band_of(chip_at(zl, 1), c)
    down = band_of(chip_at(zl, -1), c)
    across = band_of((1 - zl) * YN + y, c)
    twin = band_of(q, 1 - c)

    def remote(src, dst, send, recv, band, dom):
        return pltpu.make_async_remote_copy(
            src_ref=src, dst_ref=dst, send_sem=send, recv_sem=recv,
            device_id=(band, dom), device_id_type=MESH,
        )

    barrier = pltpu.get_barrier_semaphore()

    def greet(band, dom):
        pl.semaphore_signal(barrier, inc=1, device_id=(band, dom), device_id_type=MESH)

    for k in range(1, 16):
        greet(b, lax.rem(d + k, 16))
    for k in range(16):
        greet(twin, lax.rem(d + k, 16))
    for band in (up, down, across):
        greet(band, d)
    pl.semaphore_wait(barrier, 34)

    keep = pltpu.make_async_copy(states.at[:, pl.ds(4 * c, 4)], rows.at[c], local.at[0])

    started = []

    def spread(side, column, slot_x):
        return pl.ds(pl.multiple_of(((1 - side) * XN + slot_x) * TILE, TILE), TILE)

    wide = []
    for side in (-1, 1, 0):
        row = lax.rem(h + side + HN, HN)
        for k in range(XN):
            column = lax.rem(x + k, XN)
            if side == 0 and k == 0:
                continue
            wide.append((side, row, column))
    for n, (side, row, column) in enumerate(wide):
        slot = (1 - side) * XN + x
        copy = remote(
            window.at[column], even.at[:, spread(side, column, x), :],
            send_w.at[n], recv_w.at[slot], b, row * XN + column,
        )
        copy.start()
        started.append(copy)
    for n, (side, row, column) in enumerate(wide):
        slot = (1 - side) * XN + x
        copy = remote(
            potential, pot.at[:, spread(side, column, x), :],
            send_p.at[n], recv_p.at[slot], b, row * XN + column,
        )
        copy.start()
        started.append(copy)
    own = [
        pltpu.make_async_copy(window.at[x], even.at[:, spread(0, x, x), :], local.at[1]),
        pltpu.make_async_copy(potential, pot.at[:, spread(0, x, x), :], local.at[2]),
    ]
    for copy in own:
        copy.start()
    swap = remote(
        states.at[:, pl.ds(4 * (1 - c), 4)], rows.at[c], send_s, recv_s, twin, d
    )
    swap.start()
    keep.start()
    started.append(swap)
    keep.wait()
    swap.wait_recv()

    flat_rows = rows.reshape(2 * 128 * 32, NY)

    def split_states(k, carry):
        value = flat_rows[pl.ds(k, 256, stride=32), :]
        upper = value.astype(jnp.bfloat16)
        lanes = pl.ds(pl.multiple_of(k * NY, NY), NY)
        high[:, lanes] = upper
        low[:, lanes] = (value - upper.astype(jnp.float32)).astype(jnp.bfloat16)
        return carry

    lax.fori_loop(0, 32, split_states, 0)

    for copy in own:
        copy.wait()
    for side, row, column in wide:
        slot = (1 - side) * XN + column
        spot = spread(side, column, column)
        remote(window.at[0], even.at[:, spot, :], send_w.at[0], recv_w.at[slot], b, d).wait_recv()
        remote(potential, pot.at[:, spot, :], send_p.at[0], recv_p.at[slot], b, d).wait_recv()

    for z in range(NZ):
        product, value = apply_h(even, pot, z, 8, 88)
        odd[z, 8:88, :] = (product - CENTRE * value) * (1.0 / HALF_WIDTH)
    for source, target, first, last in ((odd, even, 8, 88), (even, odd, 16, 80), (odd, even, 24, 72)):
        for z in range(NZ):
            product, value = apply_h(source, pot, z, first, last)
            target[z, first:last, :] = (
                (product - CENTRE * value) * (2.0 / HALF_WIDTH) - target[z, first:last, :]
            )

    name = c * XN + x

    def hand_on(kind, source, offset):
        for k in range(XN):
            column = lax.rem(x + k, XN)
            for j in range(2):
                core = lax.rem(c + j, 2)
                planes = pl.ds(pl.multiple_of(offset + TILE * column, TILE), TILE)
                piece = source.at[pl.ds(4 * core, 4), planes, :]
                n = (kind * XN + k) * 2 + j
                if k == 0 and j == 0:
                    copy = pltpu.make_async_copy(piece, pieces.at[name, kind], local.at[3 + kind])
                    copy.start()
                    own_pieces.append(copy)
                else:
                    copy = remote(
                        piece, pieces.at[name, kind], send_b.at[n], recv_b.at[name, kind],
                        band_of(q, core), h * XN + column,
                    )
                    copy.start()
                    started.append(copy)

    own_pieces = []
    hand_on(0, even, 32)
    for z in range(NZ):
        product, value = apply_h(even, pot, z, 32, 64)
        image[z] = product
    hand_on(1, image, 0)

    def unit(chip, kind, half):
        return gathered.at[chip, pl.ds(8 * kind, 8), pl.ds(2048 * half, 2048)]

    def forward(chip, kind, half, sems, band):
        place = unit(chip, kind, half)
        copy = remote(place, place, sems.at[chip, kind, half], recv_g.at[chip, kind, half], band, d)
        copy.start()
        started.append(copy)

    def arrive(chip, kind, half):
        place = unit(chip, kind, half)
        remote(
            place, place, send_z.at[chip, kind, half], recv_g.at[chip, kind, half], across, d
        ).wait_recv()

    flat_pieces = pieces.reshape(8 * 64, NY)

    for kind in range(2):
        own_pieces[kind].wait()
        for k in range(XN):
            for j in range(2):
                if k == 0 and j == 0:
                    continue
                source = lax.rem(c + j, 2) * XN + lax.rem(x + k, XN)
                remote(
                    image.at[pl.ds(0, 4), pl.ds(0, 8), :], pieces.at[source, kind],
                    send_b.at[0], recv_b.at[source, kind], b, d,
                ).wait_recv()
        for k in range(32):
            gathered[q, 8 * kind : 8 * kind + 8, k * NY : (k + 1) * NY] = flat_pieces[
                pl.ds(kind * 32 + k, 8, stride=64), :
            ]
        for half in range(2):
            if kind == 0:
                forward(q, 0, half, send_z, across)
            forward(q, kind, half, send_up, up)
            forward(q, kind, half, send_down, down)
            if kind == 1:
                forward(q, 1, half, send_z, across)

    other = chip_at(1 - zl, 0)
    for half in range(2):
        arrive(other, 0, half)
        forward(other, 0, half, send_up, up)
        forward(other, 0, half, send_down, down)

    def multiply(chips):
        count = 16 * len(chips)
        for n, chip in enumerate(chips):
            for k in range(8):
                lanes = slice(512 * k, 512 * (k + 1))
                value = gathered[chip, :, lanes]
                upper = value.astype(jnp.bfloat16)
                left[16 * n : 16 * n + 16, lanes] = upper
                left[count + 16 * n : count + 16 * n + 16, lanes] = (
                    value - upper.astype(jnp.float32)
                ).astype(jnp.bfloat16)
        dims = (((1,), (1,)), ((), ()))
        both = lax.dot_general(
            left[0 : 2 * count, :], high[...], dims, preferred_element_type=jnp.float32
        )
        rest = lax.dot_general(
            left[0:count, :], low[...], dims, preferred_element_type=jnp.float32
        )
        product = both[0:count] + (both[count:] + rest)
        for n, chip in enumerate(chips):
            partial[chip] = product[16 * n : 16 * n + 16]
            for core in range(2):
                copy = remote(
                    partial.at[chip, :, pl.ds(128 * core, 128)], parts.at[d * 2 + c],
                    send_r.at[chip, core], recv_r.at[d * 2 + c], band_of(q, core), chip,
                )
                away = jnp.logical_or(chip != d, c != core)
                pl.when(away)(copy.start)
                guarded.append((away, copy))

    guarded = []

    def ring_step(step):
        for kind, mine in ((0, True), (1, True), (0, False)):
            for half in range(2):
                for direction in (1, -1):
                    keeps = half == (0 if direction == 1 else 1)
                    if step == 4 and not keeps:
                        continue
                    lo = zl if mine else 1 - zl
                    chip = chip_at(lo, -direction * step)
                    arrive(chip, kind, half)
                    if step < 3 or (step == 3 and keeps):
                        if direction == 1:
                            forward(chip, kind, half, send_up, up)
                        else:
                            forward(chip, kind, half, send_down, down)
                    if kind == 1:
                        forward(chip, kind, half, send_z, across)

    def cross(offset):
        for half in range(2):
            arrive(chip_at(1 - zl, offset), 1, half)

    ring_step(1)
    cross(0)
    multiply([q, other])
    for step in range(2, 5):
        ring_step(step)
        cross(step - 1)
        cross(1 - step)
        multiply([chip_at(lo, o) for lo in (zl, 1 - zl) for o in (step - 1, 1 - step)])
    cross(4)
    multiply([chip_at(zl, 4), chip_at(1 - zl, 4)])

    for j in range(2):
        for k in range(16):
            if j == 0 and k == 0:
                continue
            source = lax.rem(d + k, 16) * 2 + lax.rem(c + j, 2)
            remote(
                partial.at[0, :, pl.ds(0, 128)], parts.at[source],
                send_r.at[0, 0], recv_r.at[source], b, d,
            ).wait_recv()
    total = partial[d, :, pl.ds(pl.multiple_of(128 * c, 128), 128)]
    for j in range(2):
        for k in range(16):
            if j == 0 and k == 0:
                continue
            total = total + parts[lax.rem(d + k, 16) * 2 + lax.rem(c + j, 2)]
    whole[d] = total
    for k in range(1, 16):
        copy = remote(
            whole.at[d], whole.at[d], send_o.at[k], recv_o.at[d], b, lax.rem(d + k, 16)
        )
        copy.start()
        started.append(copy)
    for k in range(1, 16):
        source = lax.rem(d + k, 16)
        remote(
            whole.at[source], whole.at[source], send_o.at[k], recv_o.at[source], b, d
        ).wait_recv()
    out_f[...] = whole[:, 0:8, :].reshape(128, 128).T
    out_h[...] = whole[:, 8:16, :].reshape(128, 128).T

    for copy in started:
        copy.wait_send()
    for away, copy in guarded:
        pl.when(away)(copy.wait_send)


def per_device(states, window, potential):
    f32 = jnp.float32
    dma = pltpu.SemaphoreType.DMA
    vmem = pltpu.VMEM
    return pl.pallas_call(
        kernel,
        out_shape=(
            jax.ShapeDtypeStruct((128, 128), f32),
            jax.ShapeDtypeStruct((128, 128), f32),
        ),
        in_specs=[pl.BlockSpec(memory_space=pl.ANY)] * 3,
        out_specs=(pl.BlockSpec(memory_space=pltpu.VMEM),) * 2,
        scratch_shapes=[
            vmem((NZ, SPAN, NY), f32),
            vmem((NZ, SPAN, NY), f32),
            vmem((NZ, SPAN, NY), f32),
            vmem((NZ, 32, NY), f32),
            vmem((8, 2, 4, TILE, NY), f32),
            vmem((2, 128, 4, TILE, NY), f32),
            vmem((256, CELLS), jnp.bfloat16),
            vmem((256, CELLS), jnp.bfloat16),
            vmem((16, 16, CELLS), f32),
            vmem((128, CELLS), jnp.bfloat16),
            vmem((16, 16, 256), f32),
            vmem((32, 16, 128), f32),
            vmem((16, 16, 128), f32),
            dma((12,)), dma((12,)), dma((12,)), dma((12,)),
            dma((5,)), dma, dma,
            dma((16,)), dma((8, 2)),
            dma((16, 2, 2)), dma((16, 2, 2)), dma((16, 2, 2)), dma((16, 2, 2)),
            dma((16, 2)), dma((32,)), dma((16,)), dma((16,)),
        ],
        compiler_params=pltpu.CompilerParams(
            collective_id=0, has_side_effects=True, vmem_limit_bytes=60 * 1024 * 1024
        ),
    )(states, window, potential)


def solution(mesh):
    in_specs = (P("band", None, "dom", None), P("band", None, "dom", None), P(None, "dom", None))
    out_specs = (P("band", None), P("band", None))
    return jax.shard_map(
        per_device, mesh=mesh, in_specs=in_specs, out_specs=out_specs, check_vma=False
    )
```

time: 373 us -> 96.6 us (0.26)
  the two profiles are of different devices: /device:TPU:16 before, /device:TPU:1 now
where the time goes in v1:
time: 96.6 us; the launch traced here: 95.9 us
  Pallas kernels  92.3 us (96%)
  local copies, waits for them, and re-layouts  2.95 us (3%)
    pallas_call x1, Pallas kernels, per_device(): pl.pallas_call(kernel, out_shape=(jax.ShapeDtypeStruct((128, 128), f32),...  92.3 us
    unnamed x2, local copies, waits for them, and re-layouts  2.95 us

profile of v1, /device:TPU:1, one launch (start us, length us, event | category | flops | bytes accessed | tf_op | source)
XLA Modules:
  0.0 95.9 jit_solution(1798654228776309534)
XLA Ops:
  0.6 92.3 %shard_map.50 = (f32[128,128]{1,0:T(8,128)}, f32[128,128]{1,0:T(8,128)}) custom-call(f32[128,8,8,128]{3,2,1,0:T(8,128)} %states.1, f32[4,8,8,128]{3,2,1,0:T(8,128)} %window.1, f32[8,8,128]{2,1,0:T(8,128)} %potential.1), custom_call_target="tpu_custom_call" | custom-call | tf_op jit(solution)/shard_map/pallas_call | solution.py:345
  93.0 1.5 %copy.7 = f32[128,128]{1,0:T(8,128)} copy(f32[128,128]{1,0:T(8,128)} %get-tuple-element.4) | data formatting | bytes 131072
  94.5 1.5 %copy.8 = f32[128,128]{1,0:T(8,128)} copy(f32[128,128]{1,0:T(8,128)} %get-tuple-element.5) | data formatting | bytes 131072

commit v2 on v1

v2 whole, which is shorter than its diff:
```python
import jax
import jax.numpy as jnp
from jax import lax
from jax.experimental import pallas as pl
from jax.experimental.pallas import tpu as pltpu
from jax.sharding import PartitionSpec as P

COEFFS = (
    -5369.0 / 1800.0,
    12.0 / 7.0,
    -15.0 / 56.0,
    10.0 / 189.0,
    -1.0 / 112.0,
    2.0 / 1925.0,
    -1.0 / 16632.0,
)
CENTRE = 9.0
HALF_WIDTH = 7.0
MESH = pl.DeviceIdType.MESH
NY = 128
NZ = 8
TILE = 8
XN = 4
HN = 4
YN = 8
SPAN = 96
CELLS = 4096


def apply_h(source, potential, z, low, high):
    value = source[z, low:high, :]
    total = (3.0 * COEFFS[0]) * value
    for k in range(1, 7):
        beside = source[z, low + k : high + k, :] + source[z, low - k : high - k, :]
        beside = beside + pltpu.roll(value, k, 1) + pltpu.roll(value, NY - k, 1)
        if z + k < NZ:
            beside = beside + source[z + k, low:high, :]
        if z - k >= 0:
            beside = beside + source[z - k, low:high, :]
        total = total + COEFFS[k] * beside
    return -0.5 * total + potential[z, low:high, :] * value, value


def kernel(
    states, window, potential, out,
    even, odd, pot, image, rows, high, low, gathered, left, partial, parts, whole,
    send_w, recv_w, send_p, recv_p, send_t, recv_t, local, send_s, recv_s, send_b, recv_b,
    send_up, send_down, send_z, recv_g, send_r, recv_r, send_o, recv_o,
):
    b = lax.axis_index("band")
    d = lax.axis_index("dom")
    c = lax.rem(b, 2)
    q = lax.div(b, 2)
    y = lax.rem(q, YN)
    zl = lax.div(q, YN)
    x = lax.rem(d, XN)
    h = lax.div(d, XN)

    def band_of(chip, core):
        return chip * 2 + core

    def chip_at(lo, offset):
        return lo * YN + lax.rem(y + offset + YN, YN)

    up = band_of(chip_at(zl, 1), c)
    down = band_of(chip_at(zl, -1), c)
    across = band_of((1 - zl) * YN + y, c)
    twin = band_of(q, 1 - c)
    columns = [lax.rem(x + k, XN) for k in range(XN)]

    def remote(src, dst, send, recv, band, dom):
        return pltpu.make_async_remote_copy(
            src_ref=src, dst_ref=dst, send_sem=send, recv_sem=recv,
            device_id=(band, dom), device_id_type=MESH,
        )

    wide = []
    for side in (-1, 1, 0):
        row = lax.rem(h + side + HN, HN)
        for k in range(XN):
            if side != 0 or k != 0:
                wide.append((side, row, columns[k]))
    barrier = pltpu.get_barrier_semaphore()

    def greet(band, dom):
        pl.semaphore_signal(barrier, inc=1, device_id=(band, dom), device_id_type=MESH)

    for side, row, column in wide:
        greet(b, row * XN + column)
    for k in range(XN):
        greet(twin, h * XN + columns[k])
    for band in (up, down, across):
        greet(band, d)
    pl.semaphore_wait(barrier, 18)

    started = []

    def begin(copy):
        copy.start()
        started.append(copy)

    def planes(side, slot_x):
        return pl.ds(pl.multiple_of(((1 - side) * XN + slot_x) * TILE, TILE), TILE)

    mine = pl.ds(4 * c, 4)

    def met(side, column):
        if side == 1:
            return column != 0
        return column != XN - 1

    guarded = []
    for n, (side, row, column) in enumerate(wide):
        copy = remote(
            potential.at[mine], pot.at[mine, planes(side, x), :],
            send_p.at[n], recv_p.at[(1 - side) * XN + x], b, row * XN + column,
        )
        if side == 0:
            begin(copy)
        else:
            sent = met(side, x)
            pl.when(sent)(copy.start)
            guarded.append((sent, copy))
    for n, (side, row, column) in enumerate(wide):
        begin(
            remote(
                window.at[column], even.at[:, planes(side, x), :],
                send_w.at[n], recv_w.at[(1 - side) * XN + x], b, row * XN + column,
            )
        )
    own = [
        pltpu.make_async_copy(window.at[x], even.at[:, planes(0, x), :], local.at[1]),
        pltpu.make_async_copy(potential.at[mine], pot.at[mine, planes(0, x), :], local.at[2]),
    ]
    for copy in own:
        copy.start()
    keep = pltpu.make_async_copy(states.at[:, mine], rows.at[c], local.at[0])
    keep.start()
    swap = remote(states.at[:, pl.ds(4 * (1 - c), 4)], rows.at[c], send_s, recv_s, twin, d)
    begin(swap)

    flat_rows = rows.reshape(2 * 128 * 32, NY)

    def split_states(core):
        def body(k, carry):
            value = flat_rows[pl.ds(core * 4096 + k, 128, stride=32), :].T
            upper = value.astype(jnp.bfloat16)
            cells = pl.ds(pl.multiple_of(k * NY, NY), NY)
            lanes = pl.ds(pl.multiple_of(core * 128, 128), 128)
            high[cells, lanes] = upper
            low[cells, lanes] = (value - upper.astype(jnp.float32)).astype(jnp.bfloat16)
            return carry

        lax.fori_loop(0, 32, body, 0)

    keep.wait()
    split_states(c)

    own[1].wait()
    for n, side in enumerate((-1, 1, 0)):
        for place, row, column in wide:
            if place != side:
                continue
            copy = remote(
                potential.at[mine], pot.at[mine, planes(side, column), :],
                send_p.at[0], recv_p.at[(1 - side) * XN + column], b, d,
            )
            if side == 0:
                copy.wait_recv()
            else:
                pl.when(met(side, column))(copy.wait_recv)
        low_row, high_row = {1: (8, 32), 0: (32, 64), -1: (64, 88)}[side]
        strip = pot.at[mine, pl.ds(low_row, high_row - low_row), :]
        begin(remote(strip, strip, send_t.at[n], recv_t.at[n], twin, d))

    own[0].wait()
    for side, row, column in wide:
        remote(
            window.at[0], even.at[:, planes(side, column), :],
            send_w.at[0], recv_w.at[(1 - side) * XN + column], b, d,
        ).wait_recv()
    for n, side in enumerate((-1, 1, 0)):
        low_row, high_row = {1: (8, 32), 0: (32, 64), -1: (64, 88)}[side]
        strip = pot.at[pl.ds(4 * (1 - c), 4), pl.ds(low_row, high_row - low_row), :]
        remote(strip, strip, send_t.at[n], recv_t.at[n], twin, d).wait_recv()

    for z in range(NZ):
        product, value = apply_h(even, pot, z, 8, 88)
        odd[z, 8:88, :] = (product - CENTRE * value) * (1.0 / HALF_WIDTH)
    for source, target, first, last in ((odd, even, 8, 88), (even, odd, 16, 80), (odd, even, 24, 72)):
        for z in range(NZ):
            product, value = apply_h(source, pot, z, first, last)
            target[z, first:last, :] = (
                (product - CENTRE * value) * (2.0 / HALF_WIDTH) - target[z, first:last, :]
            )

    own_pieces = []

    def hand_on(kind, source, offset):
        for k in (0, 2, 1, 3):
            for j in range(2):
                core = lax.rem(c + j, 2)
                place = pl.ds(pl.multiple_of(offset + TILE * columns[k], TILE), TILE)
                piece = source.at[pl.ds(4 * core, 4), place, :]
                goal = gathered.at[q, kind, x, c]
                if k == 0 and j == 0:
                    copy = pltpu.make_async_copy(piece, goal, local.at[3 + kind])
                    copy.start()
                    own_pieces.append(copy)
                else:
                    begin(
                        remote(
                            piece, goal, send_b.at[kind, k, j], recv_b.at[kind, x, c],
                            band_of(q, core), h * XN + columns[k],
                        )
                    )

    hand_on(0, even, 32)
    for z in range(NZ):
        product, value = apply_h(even, pot, z, 32, 64)
        image[z] = product
    hand_on(1, image, 0)

    def forward(chip, kind, k, sems, band):
        place = gathered.at[chip, kind, columns[k]]
        begin(
            remote(place, place, sems.at[chip, kind, k], recv_g.at[chip, kind, k], band, d)
        )

    def arrive(chip, kind, k):
        place = gathered.at[chip, kind, columns[k]]
        remote(
            place, place, send_z.at[chip, kind, k], recv_g.at[chip, kind, k], across, d
        ).wait_recv()

    order = ((0, 0), (0, 1), (0, 3), (1, 0), (0, 2), (1, 1), (1, 3), (1, 2))
    for kind, k in order:
        for j in range(2):
            if k == 0 and j == 0:
                own_pieces[kind].wait()
                continue
            core = lax.rem(c + j, 2)
            remote(
                image.at[pl.ds(0, 4), pl.ds(0, TILE), :], gathered.at[q, kind, columns[k], core],
                send_b.at[0, 0, 0], recv_b.at[kind, columns[k], core], b, d,
            ).wait_recv()
        if kind == 0:
            forward(q, 0, k, send_z, across)
        forward(q, kind, k, send_up, up)
        forward(q, kind, k, send_down, down)
        if kind == 1:
            forward(q, 1, k, send_z, across)

    other = chip_at(1 - zl, 0)
    for k in (0, 1, 3, 2):
        arrive(other, 0, k)
        forward(other, 0, k, send_up, up)
        forward(other, 0, k, send_down, down)

    swap.wait_recv()
    split_states(1 - c)

    flat_pieces = gathered.reshape(16 * 512, NY)

    def multiply(chips):
        count = 16 * len(chips)
        for n, chip in enumerate(chips):
            for k in range(32):
                lanes = slice(NY * k, NY * (k + 1))
                value = flat_pieces[pl.ds(chip * 512 + k, 16, stride=32), :]
                upper = value.astype(jnp.bfloat16)
                left[16 * n : 16 * n + 16, lanes] = upper
                left[count + 16 * n : count + 16 * n + 16, lanes] = (
                    value - upper.astype(jnp.float32)
                ).astype(jnp.bfloat16)
        both = jnp.dot(left[0 : 2 * count, :], high[...], preferred_element_type=jnp.float32)
        rest = jnp.dot(left[0:count, :], low[...], preferred_element_type=jnp.float32)
        product = both[0:count] + (both[count:] + rest)
        for n, chip in enumerate(chips):
            partial[chip] = product[16 * n : 16 * n + 16]
            for core in range(2):
                copy = remote(
                    partial.at[chip, :, pl.ds(128 * core, 128)], parts.at[d * 2 + c],
                    send_r.at[chip, core], recv_r.at[d * 2 + c], band_of(q, core), chip,
                )
                away = jnp.logical_or(chip != d, c != core)
                pl.when(away)(copy.start)
                guarded.append((away, copy))

    def reduce_own():
        def take(source, total):
            remote(
                partial.at[0, :, pl.ds(0, 128)], parts.at[source],
                send_r.at[0, 0], recv_r.at[source], b, d,
            ).wait_recv()
            return total + parts[source]

        total = partial[d, :, pl.ds(pl.multiple_of(128 * c, 128), 128)]
        total = lax.fori_loop(
            0, 16, lambda k, t: take(lax.rem(d + k, 16) * 2 + (1 - c), t), total
        )
        total = lax.fori_loop(1, 16, lambda k, t: take(lax.rem(d + k, 16) * 2 + c, t), total)
        whole[d] = total
        for k in range(1, 16):
            remote(
                whole.at[d], whole.at[d], send_o.at[k], recv_o.at[d], b, lax.rem(d + k, 16)
            ).start()

    ahead = lax.rem(lax.rem(d, YN) - y + YN, YN)
    turn = jnp.minimum(ahead, YN - ahead) + jnp.where(lax.div(d, YN) == zl, 0, 1)

    def ring_step(step):
        units = [(zl, kind, k) for kind, k in order] + [(1 - zl, 0, k) for k in (0, 1, 3, 2)]
        for lo, kind, k in units:
            for direction in (1, -1):
                keeps = (k < 2) == (direction == 1)
                if step == 4 and not keeps:
                    continue
                chip = chip_at(lo, -direction * step)
                arrive(chip, kind, k)
                if step < 3 or (step == 3 and keeps):
                    if direction == 1:
                        forward(chip, kind, k, send_up, up)
                    else:
                        forward(chip, kind, k, send_down, down)
                if kind == 1:
                    forward(chip, kind, k, send_z, across)

    def cross(offset):
        for k in (0, 1, 3, 2):
            arrive(chip_at(1 - zl, offset), 1, k)

    multiply([q])
    for step in range(1, 5):
        ring_step(step)
        behind = [0] if step == 1 else [step - 1, 1 - step]
        for offset in behind:
            cross(offset)
        level = [4] if step == 4 else [step, -step]
        multiply([chip_at(zl, o) for o in level] + [chip_at(1 - zl, o) for o in behind])
        pl.when(turn == step - 1)(reduce_own)
    cross(4)
    multiply([chip_at(1 - zl, 4)])
    pl.when(turn >= 4)(reduce_own)
    for k in range(1, 16):
        source = lax.rem(d + k, 16)
        remote(
            whole.at[source], whole.at[source], send_o.at[k], recv_o.at[source], b, d
        ).wait_recv()
    out[...] = whole[...]

    for copy in started:
        copy.wait_send()
    for sent, copy in guarded:
        pl.when(sent)(copy.wait_send)
    for k in range(1, 16):
        remote(
            whole.at[d], whole.at[d], send_o.at[k], recv_o.at[d], b, lax.rem(d + k, 16)
        ).wait_send()


def finish(whole, out_f, out_h, turned):
    flat = whole.reshape(256, 128)
    for kind, out in ((0, out_f), (1, out_h)):
        for column in range(XN):
            for core in range(2):
                turned[pl.ds(4 * core + column, 16, stride=8), :] = flat[
                    pl.ds(8 * kind + 2 * column + core, 16, stride=16), :
                ]
        out[...] = turned[...].T


def per_device(states, window, potential):
    f32 = jnp.float32
    dma = pltpu.SemaphoreType.DMA
    vmem = pltpu.VMEM
    whole = pl.pallas_call(
        kernel,
        out_shape=jax.ShapeDtypeStruct((16, 16, 128), f32),
        in_specs=[pl.BlockSpec(memory_space=pl.ANY)] * 3,
        out_specs=pl.BlockSpec(memory_space=pltpu.VMEM),
        scratch_shapes=[
            vmem((NZ, SPAN, NY), f32),
            vmem((NZ, SPAN, NY), f32),
            vmem((NZ, SPAN, NY), f32),
            vmem((NZ, 32, NY), f32),
            vmem((2, 128, 4, TILE, NY), f32),
            vmem((CELLS, 256), jnp.bfloat16),
            vmem((CELLS, 256), jnp.bfloat16),
            vmem((16, 2, XN, 2, 4, TILE, NY), f32),
            vmem((128, CELLS), jnp.bfloat16),
            vmem((16, 16, 256), f32),
            vmem((32, 16, 128), f32),
            vmem((16, 16, 128), f32),
            dma((12,)), dma((12,)), dma((12,)), dma((12,)), dma((3,)), dma((3,)),
            dma((5,)), dma, dma,
            dma((2, XN, 2)), dma((2, XN, 2)),
            dma((16, 2, XN)), dma((16, 2, XN)), dma((16, 2, XN)), dma((16, 2, XN)),
            dma((16, 2)), dma((32,)), dma((16,)), dma((16,)),
        ],
        compiler_params=pltpu.CompilerParams(
            collective_id=0, has_side_effects=True, vmem_limit_bytes=60 * 1024 * 1024
        ),
    )(states, window, potential)
    return pl.pallas_call(
        finish,
        out_shape=(
            jax.ShapeDtypeStruct((128, 128), f32),
            jax.ShapeDtypeStruct((128, 128), f32),
        ),
        in_specs=[pl.BlockSpec(memory_space=pltpu.VMEM)],
        out_specs=(pl.BlockSpec(memory_space=pltpu.VMEM),) * 2,
        scratch_shapes=[vmem((128, 128), f32)],
    )(whole)


def solution(mesh):
    in_specs = (P("band", None, "dom", None), P("band", None, "dom", None), P(None, "dom", None))
    out_specs = (P("band", None), P("band", None))
    return jax.shard_map(
        per_device, mesh=mesh, in_specs=in_specs, out_specs=out_specs, check_vma=False
    )
```

time: 96.6 us -> 93.1 us (0.964)
  local copies, waits for them, and re-layouts: 2.95 us -> 0 us
    unnamed x2 -> x0, local copies, waits for them, and re-layouts: 2.95 us -> none
    pallas_call x1 -> x2, Pallas kernels: 92.3 us -> 91.9 us  [the longest x1 90.2 us: per_device(): pl.pallas_call(kernel, out_shape=jax.ShapeDtypeStruct((16, 16, 128), f32)...]
where the time goes in v2:
time: 93.1 us; the launch traced here: 92.6 us
  Pallas kernels  91.9 us (99%)
    pallas_call x1, Pallas kernels, per_device(): pl.pallas_call(kernel, out_shape=jax.ShapeDtypeStruct((16, 16, 128), f32)...  90.2 us

profile of v2, /device:TPU:1, one launch (start us, length us, event | category | flops | bytes accessed | tf_op | source)
XLA Modules:
  0.0 92.6 jit_solution(2479781332655598967)
XLA Ops:
  0.6 90.2 %shard_map.50.whole = f32[16,16,128]{2,1,0:T(8,128)} custom-call(f32[128,8,8,128]{3,2,1,0:T(8,128)} %states.1, f32[4,8,8,128]{3,2,1,0:T(8,128)} %window.1, f32[8,8,128]{2,1,0:T(8,128)} %potential.1), custom_call_target="tpu_custom_call" | custom-call | tf_op jit(solution)/shard_map/pallas_call | solution.py:377
  90.9 1.7 %shard_map.51 = (f32[128,128]{1,0:T(8,128)}, f32[128,128]{1,0:T(8,128)}) custom-call(f32[16,16,128]{2,1,0:T(8,128)} %shard_map.50.whole), custom_call_target="tpu_custom_call" | custom-call | tf_op jit(solution)/shard_map/pallas_call | solution.py:405

commit v3 on v2

--- a/solution.py
+++ b/solution.py
@@ -38,14 +38,17 @@
         if z - k >= 0:
             beside = beside + source[z - k, low:high, :]
         total = total + COEFFS[k] * beside
+    if potential is None:
+        return -0.5 * total, value
     return -0.5 * total + potential[z, low:high, :] * value, value
 
 
 def kernel(
     states, window, potential, out,
-    even, odd, pot, image, rows, high, low, gathered, left, partial, parts, whole,
+    even, odd, pot, image, rows, high, low, gathered, left, partial, parts, whole, near, far,
     send_w, recv_w, send_p, recv_p, send_t, recv_t, local, send_s, recv_s, send_b, recv_b,
     send_up, send_down, send_z, recv_g, send_r, recv_r, send_o, recv_o,
+    send_near, recv_near, send_far, recv_far,
 ):
     b = lax.axis_index("band")
     d = lax.axis_index("dom")
@@ -142,19 +145,23 @@
     flat_rows = rows.reshape(2 * 128 * 32, NY)
 
     def split_states(core):
-        def body(k, carry):
-            value = flat_rows[pl.ds(core * 4096 + k, 128, stride=32), :].T
-            upper = value.astype(jnp.bfloat16)
-            cells = pl.ds(pl.multiple_of(k * NY, NY), NY)
-            lanes = pl.ds(pl.multiple_of(core * 128, 128), 128)
-            high[cells, lanes] = upper
-            low[cells, lanes] = (value - upper.astype(jnp.float32)).astype(jnp.bfloat16)
+        def body(turn, carry):
+            for n in range(4):
+                k = 4 * turn + n
+                value = flat_rows[pl.ds(core * 4096 + k, 128, stride=32), :].T
+                upper = value.astype(jnp.bfloat16)
+                cells = pl.ds(pl.multiple_of(k * NY, NY), NY)
+                lanes = pl.ds(pl.multiple_of(core * 128, 128), 128)
+                high[cells, lanes] = upper
+                low[cells, lanes] = (value - upper.astype(jnp.float32)).astype(jnp.bfloat16)
             return carry
 
-        lax.fori_loop(0, 32, body, 0)
+        lax.fori_loop(0, 8, body, 0)
 
     keep.wait()
     split_states(c)
+    swap.wait_recv()
+    split_states(1 - c)
 
     own[1].wait()
     for n, side in enumerate((-1, 1, 0)):
@@ -179,14 +186,16 @@
             window.at[0], even.at[:, planes(side, column), :],
             send_w.at[0], recv_w.at[(1 - side) * XN + column], b, d,
         ).wait_recv()
+
+    for z in range(NZ):
+        product, value = apply_h(even, None, z, 8, 88)
+        odd[z, 8:88, :] = (product - CENTRE * value) * (1.0 / HALF_WIDTH)
     for n, side in enumerate((-1, 1, 0)):
         low_row, high_row = {1: (8, 32), 0: (32, 64), -1: (64, 88)}[side]
         strip = pot.at[pl.ds(4 * (1 - c), 4), pl.ds(low_row, high_row - low_row), :]
         remote(strip, strip, send_t.at[n], recv_t.at[n], twin, d).wait_recv()
-
     for z in range(NZ):
-        product, value = apply_h(even, pot, z, 8, 88)
-        odd[z, 8:88, :] = (product - CENTRE * value) * (1.0 / HALF_WIDTH)
+        odd[z, 8:88, :] += pot[z, 8:88, :] * even[z, 8:88, :] * (1.0 / HALF_WIDTH)
     for source, target, first, last in ((odd, even, 8, 88), (even, odd, 16, 80), (odd, even, 24, 72)):
         for z in range(NZ):
             product, value = apply_h(source, pot, z, first, last)
@@ -257,12 +266,9 @@
         forward(other, 0, k, send_up, up)
         forward(other, 0, k, send_down, down)
 
-    swap.wait_recv()
-    split_states(1 - c)
-
     flat_pieces = gathered.reshape(16 * 512, NY)
 
-    def multiply(chips):
+    def multiply(chips, last=False):
         count = 16 * len(chips)
         for n, chip in enumerate(chips):
             for k in range(32):
@@ -278,6 +284,8 @@
         product = both[0:count] + (both[count:] + rest)
         for n, chip in enumerate(chips):
             partial[chip] = product[16 * n : 16 * n + 16]
+            if last:
+                continue
             for core in range(2):
                 copy = remote(
                     partial.at[chip, :, pl.ds(128 * core, 128)], parts.at[d * 2 + c],
@@ -310,7 +318,7 @@
     turn = jnp.minimum(ahead, YN - ahead) + jnp.where(lax.div(d, YN) == zl, 0, 1)
 
     def ring_step(step):
-        units = [(zl, kind, k) for kind, k in order] + [(1 - zl, 0, k) for k in (0, 1, 3, 2)]
+        units = [(lo, kind, k) for lo, kind in ((zl, 1), (zl, 0), (1 - zl, 0)) for k in (0, 1, 3, 2)]
         for lo, kind, k in units:
             for direction in (1, -1):
                 keeps = (k < 2) == (direction == 1)
@@ -330,23 +338,61 @@
         for k in (0, 1, 3, 2):
             arrive(chip_at(1 - zl, offset), 1, k)
 
-    multiply([q])
     for step in range(1, 5):
         ring_step(step)
         behind = [0] if step == 1 else [step - 1, 1 - step]
         for offset in behind:
             cross(offset)
-        level = [4] if step == 4 else [step, -step]
+        level = {1: [0, 1, -1], 4: [4]}.get(step, [step, -step])
         multiply([chip_at(zl, o) for o in level] + [chip_at(1 - zl, o) for o in behind])
-        pl.when(turn == step - 1)(reduce_own)
+        if step == 2:
+            pl.when(turn <= 1)(reduce_own)
+        if step == 3:
+            pl.when(turn == 2)(reduce_own)
     cross(4)
-    multiply([chip_at(1 - zl, 4)])
-    pl.when(turn >= 4)(reduce_own)
+    final = chip_at(1 - zl, 4)
+    multiply([final], last=True)
+    for k in (2, 1, 3, 0):
+        for j in range(2):
+            core = lax.rem(c + j, 2)
+            part = partial.at[final, :, pl.ds(pl.multiple_of(128 * core, 128), 128)]
+            if k == 0 and j == 0:
+                near[x, c] = part[...]
+            else:
+                begin(
+                    remote(
+                        part, near.at[x, c], send_near.at[k, j], recv_near.at[x, c],
+                        band_of(q, core), h * XN + columns[k],
+                    )
+                )
+    pl.when(jnp.logical_or(turn == 3, turn == 4))(reduce_own)
+    for k in range(XN):
+        for j in range(2):
+            if k != 0 or j != 0:
+                core = lax.rem(c + j, 2)
+                remote(
+                    near.at[x, c], near.at[columns[k], core], send_near.at[0, 1],
+                    recv_near.at[columns[k], core], b, d,
+                ).wait_recv()
+    total = near[0, 0] + near[0, 1]
+    for column in range(1, XN):
+        total = total + (near[column, 0] + near[column, 1])
+    far[h] = total
+    for k in (2, 1, 3):
+        begin(
+            remote(
+                far.at[h], far.at[h], send_far.at[k], recv_far.at[h],
+                b, lax.rem(h + k, HN) * XN + x,
+            )
+        )
     for k in range(1, 16):
         source = lax.rem(d + k, 16)
-        remote(
-            whole.at[source], whole.at[source], send_o.at[k], recv_o.at[source], b, d
-        ).wait_recv()
+        copy = remote(whole.at[source], whole.at[source], send_o.at[k], recv_o.at[source], b, d)
+        pl.when(source != final)(copy.wait_recv)
+    for k in range(1, HN):
+        row = lax.rem(h + k, HN)
+        remote(far.at[h], far.at[row], send_far.at[k], recv_far.at[row], b, d).wait_recv()
+    whole[final] = (far[0] + far[1]) + (far[2] + far[3])
     out[...] = whole[...]
 
     for copy in started:
@@ -354,9 +400,8 @@
     for sent, copy in guarded:
         pl.when(sent)(copy.wait_send)
     for k in range(1, 16):
-        remote(
-            whole.at[d], whole.at[d], send_o.at[k], recv_o.at[d], b, lax.rem(d + k, 16)
-        ).wait_send()
+        copy = remote(whole.at[d], whole.at[d], send_o.at[k], recv_o.at[d], b, lax.rem(d + k, 16))
+        pl.when(d != final)(copy.wait_send)
 
 
 def finish(whole, out_f, out_h, turned):
@@ -392,11 +437,14 @@
             vmem((16, 16, 256), f32),
             vmem((32, 16, 128), f32),
             vmem((16, 16, 128), f32),
+            vmem((XN, 2, 16, 128), f32),
+            vmem((HN, 16, 128), f32),
             dma((12,)), dma((12,)), dma((12,)), dma((12,)), dma((3,)), dma((3,)),
             dma((5,)), dma, dma,
             dma((2, XN, 2)), dma((2, XN, 2)),
             dma((16, 2, XN)), dma((16, 2, XN)), dma((16, 2, XN)), dma((16, 2, XN)),
             dma((16, 2)), dma((32,)), dma((16,)), dma((16,)),
+            dma((XN, 2)), dma((XN, 2)), dma((HN,)), dma((HN,)),
         ],
         compiler_params=pltpu.CompilerParams(
             collective_id=0, has_side_effects=True, vmem_limit_bytes=60 * 1024 * 1024

time: 93.1 us -> 90.6 us (0.973)
  Pallas kernels: 91.9 us -> 89.8 us
    pallas_call x1, Pallas kernels: 90.2 us -> 88.1 us  [per_device(): pl.pallas_call(kernel, out_shape=jax.ShapeDtypeStruct((16, 16, 128), f32)...]
where the time goes in v3:
time: 90.6 us; the launch traced here: 90.5 us
  Pallas kernels  89.8 us (99%)
    pallas_call x1, Pallas kernels, per_device(): pl.pallas_call(kernel, out_shape=jax.ShapeDtypeStruct((16, 16, 128), f32)...  88.1 us

profile of v3, /device:TPU:1, one launch (start us, length us, event | category | flops | bytes accessed | tf_op | source)
XLA Modules:
  0.0 90.5 jit_solution(14379494881844516749)
XLA Ops:
  0.6 88.1 %shard_map.50.whole = f32[16,16,128]{2,1,0:T(8,128)} custom-call(f32[128,8,8,128]{3,2,1,0:T(8,128)} %states.1, f32[4,8,8,128]{3,2,1,0:T(8,128)} %window.1, f32[8,8,128]{2,1,0:T(8,128)} %potential.1), custom_call_target="tpu_custom_call" | custom-call | tf_op jit(solution)/shard_map/pallas_call | solution.py:422
  88.8 1.7 %shard_map.51 = (f32[128,128]{1,0:T(8,128)}, f32[128,128]{1,0:T(8,128)}) custom-call(f32[16,16,128]{2,1,0:T(8,128)} %shard_map.50.whole), custom_call_target="tpu_custom_call" | custom-call | tf_op jit(solution)/shard_map/pallas_call | solution.py:453

commit v4 on v3

--- a/solution.py
+++ b/solution.py
@@ -315,11 +315,13 @@
             ).start()
 
     ahead = lax.rem(lax.rem(d, YN) - y + YN, YN)
-    turn = jnp.minimum(ahead, YN - ahead) + jnp.where(lax.div(d, YN) == zl, 0, 1)
-
-    def ring_step(step):
-        units = [(lo, kind, k) for lo, kind in ((zl, 1), (zl, 0), (1 - zl, 0)) for k in (0, 1, 3, 2)]
-        for lo, kind, k in units:
+    final = chip_at(1 - zl, 4)
+    turn = jnp.where(d == final, 5, jnp.maximum(jnp.minimum(ahead, YN - ahead), 1))
+    images = ((zl, 1),)
+    filtered = ((zl, 0), (1 - zl, 0))
+
+    def ring_step(step, kinds):
+        for lo, kind, k in [(lo, kind, k) for lo, kind in kinds for k in (0, 1, 3, 2)]:
             for direction in (1, -1):
                 keeps = (k < 2) == (direction == 1)
                 if step == 4 and not keeps:
@@ -338,19 +340,19 @@
         for k in (0, 1, 3, 2):
             arrive(chip_at(1 - zl, offset), 1, k)
 
-    for step in range(1, 5):
-        ring_step(step)
-        behind = [0] if step == 1 else [step - 1, 1 - step]
-        for offset in behind:
+    for step in range(1, 4):
+        ring_step(step, images + filtered)
+        if step == 3:
+            ring_step(4, images)
+        offsets = [step, -step] if step > 1 else [0, step, -step]
+        for offset in offsets:
             cross(offset)
-        level = {1: [0, 1, -1], 4: [4]}.get(step, [step, -step])
-        multiply([chip_at(zl, o) for o in level] + [chip_at(1 - zl, o) for o in behind])
-        if step == 2:
-            pl.when(turn <= 1)(reduce_own)
-        if step == 3:
-            pl.when(turn == 2)(reduce_own)
+        multiply([chip_at(lo, o) for lo in (zl, 1 - zl) for o in offsets])
+        if step > 1:
+            pl.when(turn == step - 1)(reduce_own)
+    ring_step(4, filtered)
+    multiply([chip_at(zl, 4)])
     cross(4)
-    final = chip_at(1 - zl, 4)
     multiply([final], last=True)
     for k in (2, 1, 3, 0):
         for j in range(2):
@@ -365,7 +367,6 @@
                         band_of(q, core), h * XN + columns[k],
                     )
                 )
-    pl.when(jnp.logical_or(turn == 3, turn == 4))(reduce_own)
     for k in range(XN):
         for j in range(2):
             if k != 0 or j != 0:
@@ -385,6 +386,7 @@
                 b, lax.rem(h + k, HN) * XN + x,
             )
         )
+    pl.when(jnp.logical_or(turn == 3, turn == 4))(reduce_own)
     for k in range(1, 16):
         source = lax.rem(d + k, 16)
         copy = remote(whole.at[source], whole.at[source], send_o.at[k], recv_o.at[source], b, d)
@@ -433,7 +435,7 @@
             vmem((CELLS, 256), jnp.bfloat16),
             vmem((CELLS, 256), jnp.bfloat16),
             vmem((16, 2, XN, 2, 4, TILE, NY), f32),
-            vmem((128, CELLS), jnp.bfloat16),
+            vmem((192, CELLS), jnp.bfloat16),
             vmem((16, 16, 256), f32),
             vmem((32, 16, 128), f32),
             vmem((16, 16, 128), f32),

time: 90.6 us -> 93.3 us (1.030)
  Pallas kernels: 89.8 us -> 92.5 us
    pallas_call x1, Pallas kernels: 88.1 us -> 90.8 us  [per_device(): pl.pallas_call(kernel, out_shape=jax.ShapeDtypeStruct((16, 16, 128), f32)...]
where the time goes in v4:
time: 93.3 us; the launch traced here: 93.1 us
  Pallas kernels  92.5 us (99%)
    pallas_call x1, Pallas kernels, per_device(): pl.pallas_call(kernel, out_shape=jax.ShapeDtypeStruct((16, 16, 128), f32)...  90.8 us

profile of v4, /device:TPU:1, one launch (start us, length us, event | category | flops | bytes accessed | tf_op | source)
XLA Modules:
  0.0 93.1 jit_solution(17097648766300056930)
XLA Ops:
  0.6 90.8 %shard_map.50.whole = f32[16,16,128]{2,1,0:T(8,128)} custom-call(f32[128,8,8,128]{3,2,1,0:T(8,128)} %states.1, f32[4,8,8,128]{3,2,1,0:T(8,128)} %window.1, f32[8,8,128]{2,1,0:T(8,128)} %potential.1), custom_call_target="tpu_custom_call" | custom-call | tf_op jit(solution)/shard_map/pallas_call | solution.py:424
  91.4 1.7 %shard_map.51 = (f32[128,128]{1,0:T(8,128)}, f32[128,128]{1,0:T(8,128)}) custom-call(f32[16,16,128]{2,1,0:T(8,128)} %shard_map.50.whole), custom_call_target="tpu_custom_call" | custom-call | tf_op jit(solution)/shard_map/pallas_call | solution.py:455

commit v5 on v4

--- a/solution.py
+++ b/solution.py
@@ -316,7 +316,10 @@
 
     ahead = lax.rem(lax.rem(d, YN) - y + YN, YN)
     final = chip_at(1 - zl, 4)
-    turn = jnp.where(d == final, 5, jnp.maximum(jnp.minimum(ahead, YN - ahead), 1))
+    facing = chip_at(zl, 4)
+    apart = jnp.minimum(ahead, YN - ahead)
+    turn = jnp.where(lax.div(d, YN) == zl, jnp.maximum(apart, 1), jnp.minimum(apart + 1, 3))
+    turn = jnp.where(apart == 4, 5, turn)
     images = ((zl, 1),)
     filtered = ((zl, 0), (1 - zl, 0))
 
@@ -344,57 +347,70 @@
         ring_step(step, images + filtered)
         if step == 3:
             ring_step(4, images)
-        offsets = [step, -step] if step > 1 else [0, step, -step]
-        for offset in offsets:
+        level = [0, 1, -1] if step == 1 else [step, -step]
+        behind = {1: [0], 2: [1, -1], 3: [2, -2, 3, -3]}[step]
+        for offset in behind:
             cross(offset)
-        multiply([chip_at(lo, o) for lo in (zl, 1 - zl) for o in offsets])
+        multiply([chip_at(zl, o) for o in level] + [chip_at(1 - zl, o) for o in behind])
         if step > 1:
             pl.when(turn == step - 1)(reduce_own)
+
+    def near_start(n, chip):
+        for k in (2, 1, 3, 0):
+            for j in range(2):
+                core = lax.rem(c + j, 2)
+                part = partial.at[chip, :, pl.ds(pl.multiple_of(128 * core, 128), 128)]
+                if k == 0 and j == 0:
+                    near[n, x, c] = part[...]
+                else:
+                    begin(
+                        remote(
+                            part, near.at[n, x, c], send_near.at[n, k, j], recv_near.at[n, x, c],
+                            band_of(q, core), h * XN + columns[k],
+                        )
+                    )
+
+    def near_finish(n):
+        for k in range(XN):
+            for j in range(2):
+                if k != 0 or j != 0:
+                    core = lax.rem(c + j, 2)
+                    remote(
+                        near.at[n, x, c], near.at[n, columns[k], core], send_near.at[n, 0, 1],
+                        recv_near.at[n, columns[k], core], b, d,
+                    ).wait_recv()
+        total = near[n, 0, 0] + near[n, 0, 1]
+        for column in range(1, XN):
+            total = total + (near[n, column, 0] + near[n, column, 1])
+        far[n, h] = total
+        for k in (2, 1, 3):
+            begin(
+                remote(
+                    far.at[n, h], far.at[n, h], send_far.at[n, k], recv_far.at[n, h],
+                    b, lax.rem(h + k, HN) * XN + x,
+                )
+            )
+
     ring_step(4, filtered)
-    multiply([chip_at(zl, 4)])
+    multiply([facing], last=True)
+    near_start(0, facing)
     cross(4)
     multiply([final], last=True)
-    for k in (2, 1, 3, 0):
-        for j in range(2):
-            core = lax.rem(c + j, 2)
-            part = partial.at[final, :, pl.ds(pl.multiple_of(128 * core, 128), 128)]
-            if k == 0 and j == 0:
-                near[x, c] = part[...]
-            else:
-                begin(
-                    remote(
-                        part, near.at[x, c], send_near.at[k, j], recv_near.at[x, c],
-                        band_of(q, core), h * XN + columns[k],
-                    )
-                )
-    for k in range(XN):
-        for j in range(2):
-            if k != 0 or j != 0:
-                core = lax.rem(c + j, 2)
-                remote(
-                    near.at[x, c], near.at[columns[k], core], send_near.at[0, 1],
-                    recv_near.at[columns[k], core], b, d,
-                ).wait_recv()
-    total = near[0, 0] + near[0, 1]
-    for column in range(1, XN):
-        total = total + (near[column, 0] + near[column, 1])
-    far[h] = total
-    for k in (2, 1, 3):
-        begin(
-            remote(
-                far.at[h], far.at[h], send_far.at[k], recv_far.at[h],
-                b, lax.rem(h + k, HN) * XN + x,
-            )
-        )
-    pl.when(jnp.logical_or(turn == 3, turn == 4))(reduce_own)
+    near_start(1, final)
+    near_finish(0)
+    pl.when(turn == 3)(reduce_own)
+    near_finish(1)
     for k in range(1, 16):
         source = lax.rem(d + k, 16)
         copy = remote(whole.at[source], whole.at[source], send_o.at[k], recv_o.at[source], b, d)
-        pl.when(source != final)(copy.wait_recv)
-    for k in range(1, HN):
-        row = lax.rem(h + k, HN)
-        remote(far.at[h], far.at[row], send_far.at[k], recv_far.at[row], b, d).wait_recv()
-    whole[final] = (far[0] + far[1]) + (far[2] + far[3])
+        pl.when(jnp.logical_and(source != final, source != facing))(copy.wait_recv)
+    for n, chip in ((0, facing), (1, final)):
+        for k in range(1, HN):
+            row = lax.rem(h + k, HN)
+            remote(
+                far.at[n, h], far.at[n, row], send_far.at[n, k], recv_far.at[n, row], b, d
+            ).wait_recv()
+        whole[chip] = (far[n, 0] + far[n, 1]) + (far[n, 2] + far[n, 3])
     out[...] = whole[...]
 
     for copy in started:
@@ -403,7 +419,7 @@
         pl.when(sent)(copy.wait_send)
     for k in range(1, 16):
         copy = remote(whole.at[d], whole.at[d], send_o.at[k], recv_o.at[d], b, lax.rem(d + k, 16))
-        pl.when(d != final)(copy.wait_send)
+        pl.when(turn < 5)(copy.wait_send)
 
 
 def finish(whole, out_f, out_h, turned):
@@ -439,14 +455,14 @@
             vmem((16, 16, 256), f32),
             vmem((32, 16, 128), f32),
             vmem((16, 16, 128), f32),
-            vmem((XN, 2, 16, 128), f32),
-            vmem((HN, 16, 128), f32),
+            vmem((2, XN, 2, 16, 128), f32),
+            vmem((2, HN, 16, 128), f32),
             dma((12,)), dma((12,)), dma((12,)), dma((12,)), dma((3,)), dma((3,)),
             dma((5,)), dma, dma,
             dma((2, XN, 2)), dma((2, XN, 2)),
             dma((16, 2, XN)), dma((16, 2, XN)), dma((16, 2, XN)), dma((16, 2, XN)),
             dma((16, 2)), dma((32,)), dma((16,)), dma((16,)),
-            dma((XN, 2)), dma((XN, 2)), dma((HN,)), dma((HN,)),
+            dma((2, XN, 2)), dma((2, XN, 2)), dma((2, HN)), dma((2, HN)),
         ],
         compiler_params=pltpu.CompilerParams(
             collective_id=0, has_side_effects=True, vmem_limit_bytes=60 * 1024 * 1024

time: 93.3 us -> 89.5 us (0.959)
  Pallas kernels: 92.5 us -> 88.5 us
    pallas_call x1, Pallas kernels: 90.8 us -> 86.8 us  [per_device(): pl.pallas_call(kernel, out_shape=jax.ShapeDtypeStruct((16, 16, 128), f32)...]
where the time goes in v5:
time: 89.5 us; the launch traced here: 89.2 us
  Pallas kernels  88.5 us (99%)
    pallas_call x1, Pallas kernels, per_device(): pl.pallas_call(kernel, out_shape=jax.ShapeDtypeStruct((16, 16, 128), f32)...  86.8 us

profile of v5, /device:TPU:1, one launch (start us, length us, event | category | flops | bytes accessed | tf_op | source)
XLA Modules:
  0.0 89.2 jit_solution(11287914487457846268)
XLA Ops:
  0.6 86.8 %shard_map.50.whole = f32[16,16,128]{2,1,0:T(8,128)} custom-call(f32[128,8,8,128]{3,2,1,0:T(8,128)} %states.1, f32[4,8,8,128]{3,2,1,0:T(8,128)} %window.1, f32[8,8,128]{2,1,0:T(8,128)} %potential.1), custom_call_target="tpu_custom_call" | custom-call | tf_op jit(solution)/shard_map/pallas_call | solution.py:440
  87.5 1.7 %shard_map.51 = (f32[128,128]{1,0:T(8,128)}, f32[128,128]{1,0:T(8,128)}) custom-call(f32[16,16,128]{2,1,0:T(8,128)} %shard_map.50.whole), custom_call_target="tpu_custom_call" | custom-call | tf_op jit(solution)/shard_map/pallas_call | solution.py:471

commit v6 on v5

--- a/solution.py
+++ b/solution.py
@@ -125,12 +125,13 @@
             pl.when(sent)(copy.start)
             guarded.append((sent, copy))
     for n, (side, row, column) in enumerate(wide):
-        begin(
-            remote(
-                window.at[column], even.at[:, planes(side, x), :],
-                send_w.at[n], recv_w.at[(1 - side) * XN + x], b, row * XN + column,
+        if side == 0 or n % XN != 2:
+            begin(
+                remote(
+                    window.at[column], even.at[:, planes(side, x), :],
+                    send_w.at[n], recv_w.at[(1 - side) * XN + x], b, row * XN + column,
+                )
             )
-        )
     own = [
         pltpu.make_async_copy(window.at[x], even.at[:, planes(0, x), :], local.at[1]),
         pltpu.make_async_copy(potential.at[mine], pot.at[mine, planes(0, x), :], local.at[2]),
@@ -160,6 +161,18 @@
 
     keep.wait()
     split_states(c)
+    distant = columns[2]
+    tile = even.at[:, planes(0, distant), :]
+    remote(window.at[0], tile, send_w.at[0], recv_w.at[XN + distant], b, d).wait_recv()
+    passed = []
+    for n, side in ((2, -1), (6, 1)):
+        copy = remote(
+            tile, even.at[:, planes(side, distant), :],
+            send_w.at[n], recv_w.at[(1 - side) * XN + distant],
+            b, lax.rem(h + side + HN, HN) * XN + x,
+        )
+        copy.start()
+        passed.append(copy)
     swap.wait_recv()
     split_states(1 - c)
 
@@ -181,7 +194,9 @@
         begin(remote(strip, strip, send_t.at[n], recv_t.at[n], twin, d))
 
     own[0].wait()
-    for side, row, column in wide:
+    for n, (side, row, column) in enumerate(wide):
+        if side == 0 and n == 9:
+            continue
         remote(
             window.at[0], even.at[:, planes(side, column), :],
             send_w.at[0], recv_w.at[(1 - side) * XN + column], b, d,
@@ -196,6 +211,8 @@
         remote(strip, strip, send_t.at[n], recv_t.at[n], twin, d).wait_recv()
     for z in range(NZ):
         odd[z, 8:88, :] += pot[z, 8:88, :] * even[z, 8:88, :] * (1.0 / HALF_WIDTH)
+    for copy in passed:
+        copy.wait_send()
     for source, target, first, last in ((odd, even, 8, 88), (even, odd, 16, 80), (odd, even, 24, 72)):
         for z in range(NZ):
             product, value = apply_h(source, pot, z, first, last)
@@ -318,8 +335,8 @@
     final = chip_at(1 - zl, 4)
     facing = chip_at(zl, 4)
     apart = jnp.minimum(ahead, YN - ahead)
-    turn = jnp.where(lax.div(d, YN) == zl, jnp.maximum(apart, 1), jnp.minimum(apart + 1, 3))
-    turn = jnp.where(apart == 4, 5, turn)
+    turn = jnp.where(lax.div(d, YN) == zl, jnp.maximum(apart, 1), jnp.minimum(apart + 1, 2))
+    turn = jnp.where(apart == 3, 3, jnp.where(apart == 4, 5, turn))
     images = ((zl, 1),)
     filtered = ((zl, 0), (1 - zl, 0))
 
@@ -343,17 +360,24 @@
         for k in (0, 1, 3, 2):
             arrive(chip_at(1 - zl, offset), 1, k)
 
+    def pair(lo, offset):
+        return [chip_at(lo, offset), chip_at(lo, -offset)]
+
     for step in range(1, 4):
-        ring_step(step, images + filtered)
+        ring_step(step, images)
+        if step > 1:
+            cross(step - 1)
+            cross(1 - step)
+            multiply(pair(1 - zl, step - 1))
+        ring_step(step, filtered)
+        if step == 1:
+            cross(0)
+            multiply([q, other] + pair(zl, 1))
+            continue
         if step == 3:
             ring_step(4, images)
-        level = [0, 1, -1] if step == 1 else [step, -step]
-        behind = {1: [0], 2: [1, -1], 3: [2, -2, 3, -3]}[step]
-        for offset in behind:
-            cross(offset)
-        multiply([chip_at(zl, o) for o in level] + [chip_at(1 - zl, o) for o in behind])
-        if step > 1:
-            pl.when(turn == step - 1)(reduce_own)
+        multiply(pair(zl, step))
+        pl.when(turn == step - 1)(reduce_own)
 
     def near_start(n, chip):
         for k in (2, 1, 3, 0):
@@ -391,14 +415,16 @@
                 )
             )
 
+    cross(3)
+    cross(-3)
+    multiply(pair(1 - zl, 3))
     ring_step(4, filtered)
-    multiply([facing], last=True)
+    cross(4)
+    multiply([facing, final], last=True)
     near_start(0, facing)
-    cross(4)
-    multiply([final], last=True)
     near_start(1, final)
+    pl.when(turn == 3)(reduce_own)
     near_finish(0)
-    pl.when(turn == 3)(reduce_own)
     near_finish(1)
     for k in range(1, 16):
         source = lax.rem(d + k, 16)

time: 89.5 us -> 89.1 us (level)
  no operation moved by 1% of the time
where the time goes in v6:
time: 89.1 us; the launch traced here: 88.9 us
  Pallas kernels  88.3 us (99%)
    pallas_call x1, Pallas kernels, per_device(): pl.pallas_call(kernel, out_shape=jax.ShapeDtypeStruct((16, 16, 128), f32)...  86.6 us

profile of v6, /device:TPU:1, one launch (start us, length us, event | category | flops | bytes accessed | tf_op | source)
XLA Modules:
  0.0 88.9 jit_solution(12114529015619438398)
XLA Ops:
  0.6 86.6 %shard_map.50.whole = f32[16,16,128]{2,1,0:T(8,128)} custom-call(f32[128,8,8,128]{3,2,1,0:T(8,128)} %states.1, f32[4,8,8,128]{3,2,1,0:T(8,128)} %window.1, f32[8,8,128]{2,1,0:T(8,128)} %potential.1), custom_call_target="tpu_custom_call" | custom-call | tf_op jit(solution)/shard_map/pallas_call | solution.py:466
  87.2 1.7 %shard_map.51 = (f32[128,128]{1,0:T(8,128)}, f32[128,128]{1,0:T(8,128)}) custom-call(f32[16,16,128]{2,1,0:T(8,128)} %shard_map.50.whole), custom_call_target="tpu_custom_call" | custom-call | tf_op jit(solution)/shard_map/pallas_call | solution.py:497

commit v7 on v6

--- a/solution.py
+++ b/solution.py
@@ -223,7 +223,7 @@
     own_pieces = []
 
     def hand_on(kind, source, offset):
-        for k in (0, 2, 1, 3):
+        for k in (0, 1, 3, 2):
             for j in range(2):
                 core = lax.rem(c + j, 2)
                 place = pl.ds(pl.multiple_of(offset + TILE * columns[k], TILE), TILE)

time: 89.1 us -> 88.9 us (level)
  no operation moved by 1% of the time
where the time goes in v7:
time: 88.9 us; the launch traced here: 88.8 us
  Pallas kernels  88.1 us (99%)
    pallas_call x1, Pallas kernels, per_device(): pl.pallas_call(kernel, out_shape=jax.ShapeDtypeStruct((16, 16, 128), f32)...  86.4 us

profile of v7, /device:TPU:1, one launch (start us, length us, event | category | flops | bytes accessed | tf_op | source)
XLA Modules:
  0.0 88.8 jit_solution(6164028996367343932)
XLA Ops:
  0.6 86.4 %shard_map.50.whole = f32[16,16,128]{2,1,0:T(8,128)} custom-call(f32[128,8,8,128]{3,2,1,0:T(8,128)} %states.1, f32[4,8,8,128]{3,2,1,0:T(8,128)} %window.1, f32[8,8,128]{2,1,0:T(8,128)} %potential.1), custom_call_target="tpu_custom_call" | custom-call | tf_op jit(solution)/shard_map/pallas_call | solution.py:466
  87.1 1.7 %shard_map.51 = (f32[128,128]{1,0:T(8,128)}, f32[128,128]{1,0:T(8,128)}) custom-call(f32[16,16,128]{2,1,0:T(8,128)} %shard_map.50.whole), custom_call_target="tpu_custom_call" | custom-call | tf_op jit(solution)/shard_map/pallas_call | solution.py:497
